TPU v7x, 32 devices: a whole 2x2x4 slice. The times are simulated.
32 devices in a mesh: fsdp: 4 (over y, x), seq: 8 (over z, core).
Axes of the slice: x: 2, y: 2, z: 4, core: 2. Of those that a mesh axis runs over, the one named last changes fastest.
Arguments:
- residual_in: bfloat16 [4, 1024, 2048], P('fsdp', 'seq'), may hold values from -6 to 6
- attn_gain: bfloat16 [2048], replicated, may hold values from 0.5 to 1.5
- mlp_gain: bfloat16 [2048], replicated, may hold values from 0.5 to 1.5
- w_qkv: bfloat16 [2048, 3, 2048], P('fsdp'), may hold values from -0.125 to 0.125
- w_out: bfloat16 [2048, 2048], P('fsdp'), may hold values from -1 to 1
- w_gate_up: bfloat16 [8192, 2, 2048], P('fsdp'), may hold values from -0.125 to 0.125
- w_down: bfloat16 [2048, 8192], P('fsdp'), may hold values from -0.0625 to 0.0625
- cotangent: bfloat16 [4, 1024, 2048], P('fsdp', 'seq'), may hold values from -6 to 6
Outputs:
- layer_out: bfloat16 [4, 1024, 2048], P('fsdp', 'seq')
- grad_input: float32 [4, 1024, 2048], P('fsdp', 'seq')
- grad_attn_gain: float32 [2048], P(('fsdp', 'seq'))
- grad_mlp_gain: float32 [2048], P(('fsdp', 'seq'))
- grad_qkv: float32 [2048, 3, 2048], P(('seq', 'fsdp'))
- grad_out_proj: float32 [2048, 2048], P(None, ('seq', 'fsdp'))
- grad_gate_up: float32 [8192, 2, 2048], P(('seq', 'fsdp'))
- grad_down: float32 [2048, 8192], P(None, ('seq', 'fsdp'))
All inputs are finite; a program needn't handle non-finite values.
Results may differ from a plain program's by a relative error of at most 0.018.
Values may be sent and summed in bfloat16 or wider, within the bound.
No kernel may reach another device: no remote copies, remote signals or barrier semaphores. Data moves between devices by JAX's collectives and lax.ppermute only.
A program may use at most 384 MiB of HBM per device.

v0:
```python
import math
import jax
import jax.numpy as jnp
from jax import lax
from jax.sharding import PartitionSpec as P

HD = 64
NORM_EPS = 1e-05
ROPE_BASE = 130000.0


def rotate(matrix):
    shaped = matrix.reshape(matrix.shape[:-1] + (matrix.shape[-1] // HD, 2, HD // 2))
    turned = jnp.stack([-shaped[..., 1, :], shaped[..., 0, :]], axis=-2)
    return turned.reshape(matrix.shape)


def rotate_back(matrix):
    shaped = matrix.reshape(matrix.shape[:-1] + (matrix.shape[-1] // HD, 2, HD // 2))
    turned = jnp.stack([shaped[..., 1, :], -shaped[..., 0, :]], axis=-2)
    return turned.reshape(matrix.shape)


def rope_tables(positions, columns):
    freq_index = (jnp.arange(columns, dtype=jnp.int32) % (HD // 2)).astype(jnp.float32)
    inverse = ROPE_BASE ** (-2.0 * freq_index / HD)
    angles = positions.astype(jnp.float32)[:, None] * inverse[None, :]
    return (jnp.cos(angles), jnp.sin(angles))


def rms_scale(matrix):
    return lax.rsqrt(jnp.mean(matrix * matrix, axis=-1, keepdims=True) + NORM_EPS)


def rms_back(grad_normed, matrix, scale_rows, gain):
    weighted = grad_normed * gain
    inner_mean = jnp.mean(weighted * matrix, axis=-1, keepdims=True)
    grad_matrix = scale_rows * weighted - matrix * scale_rows**3 * inner_mean
    grad_gain = jnp.sum(grad_normed * matrix * scale_rows, axis=0)
    return (grad_matrix, grad_gain)


def attend_forward(queries, key_rows, values):
    seq_count, length, width_here = queries.shape
    heads_here = width_here // HD
    q_block = min(512, length)
    k_block = min(256, length)
    inv_root = 1.0 / math.sqrt(HD)
    shaped_q = queries.reshape(seq_count, length, heads_here, HD)
    shaped_k = key_rows.reshape(seq_count, length, heads_here, HD)
    shaped_v = values.reshape(seq_count, length, heads_here, HD)

    def query_step(q_index, carried):
        attended, totals = carried
        offset = q_index * q_block
        q_rows = lax.dynamic_slice_in_dim(shaped_q, offset, q_block, 1)
        query_pos = offset + jnp.arange(q_block, dtype=jnp.int32)

        def key_step(k_index, running):
            unnorm, denominator = running
            k_start = k_index * k_block
            k_rows = lax.dynamic_slice_in_dim(shaped_k, k_start, k_block, 1)
            v_rows = lax.dynamic_slice_in_dim(shaped_v, k_start, k_block, 1)
            scores = (
                jnp.einsum("bqhd,bkhd->bhqk", q_rows, k_rows, preferred_element_type=jnp.float32)
                * inv_root
            )
            causal = (k_start + jnp.arange(k_block, dtype=jnp.int32))[None, :] <= query_pos[:, None]
            exp_scores = jnp.where(causal, jnp.exp(scores), 0.0)
            denominator = denominator + jnp.sum(exp_scores, axis=-1)
            unnorm = unnorm + jnp.einsum(
                "bhqk,bkhd->bqhd",
                exp_scores.astype(jnp.bfloat16),
                v_rows,
                preferred_element_type=jnp.float32,
            )
            return (unnorm, denominator)

        start_state = (
            jnp.zeros((seq_count, q_block, heads_here, HD), jnp.float32),
            jnp.zeros((seq_count, heads_here, q_block), jnp.float32),
        )
        unnorm, denominator = lax.fori_loop(0, (offset + q_block) // k_block, key_step, start_state)
        block_out = unnorm / jnp.transpose(denominator, (0, 2, 1))[..., None]
        attended = lax.dynamic_update_slice_in_dim(attended, block_out, offset, 1)
        totals = lax.dynamic_update_slice_in_dim(totals, denominator, offset, 2)
        return (attended, totals)

    initial = (
        jnp.zeros((seq_count, length, heads_here, HD), jnp.float32),
        jnp.zeros((seq_count, heads_here, length), jnp.float32),
    )
    attended, totals = lax.fori_loop(0, length // q_block, query_step, initial)
    return (attended.reshape(seq_count, length, width_here), totals)


def attend_backward(queries, key_rows, values, attended, totals, grad_attended):
    seq_count, length, width_here = queries.shape
    heads_here = width_here // HD
    q_block = min(512, length)
    k_block = min(256, length)
    inv_root = 1.0 / math.sqrt(HD)
    shaped_q = queries.reshape(seq_count, length, heads_here, HD)
    shaped_k = key_rows.reshape(seq_count, length, heads_here, HD)
    shaped_v = values.reshape(seq_count, length, heads_here, HD)
    shaped_grad = grad_attended.reshape(seq_count, length, heads_here, HD).astype(jnp.float32)
    shaped_att = attended.reshape(seq_count, length, heads_here, HD)
    totals_rows = jnp.transpose(totals, (0, 2, 1))
    grad_total = -jnp.sum(shaped_grad * shaped_att, axis=-1) / totals_rows
    grad_unnorm = (shaped_grad / totals_rows[..., None]).astype(jnp.bfloat16)

    def query_step(q_index, carried):
        grad_q, grad_k, grad_v = carried
        offset = q_index * q_block
        q_rows = lax.dynamic_slice_in_dim(shaped_q, offset, q_block, 1)
        g_rows = lax.dynamic_slice_in_dim(grad_unnorm, offset, q_block, 1)
        total_rows = jnp.transpose(
            lax.dynamic_slice_in_dim(grad_total, offset, q_block, 1), (0, 2, 1)
        )
        query_pos = offset + jnp.arange(q_block, dtype=jnp.int32)

        def key_step(k_index, running):
            dq_acc, dk_all, dv_all = running
            k_start = k_index * k_block
            k_rows = lax.dynamic_slice_in_dim(shaped_k, k_start, k_block, 1)
            v_rows = lax.dynamic_slice_in_dim(shaped_v, k_start, k_block, 1)
            scores = (
                jnp.einsum("bqhd,bkhd->bhqk", q_rows, k_rows, preferred_element_type=jnp.float32)
                * inv_root
            )
            causal = (k_start + jnp.arange(k_block, dtype=jnp.int32))[None, :] <= query_pos[:, None]
            exp_scores = jnp.where(causal, jnp.exp(scores), 0.0)
            grad_prob = jnp.einsum(
                "bqhd,bkhd->bhqk", g_rows, v_rows, preferred_element_type=jnp.float32
            )
            grad_scores = (exp_scores * (grad_prob + total_rows[..., None])).astype(jnp.bfloat16)
            dq_acc = (
                dq_acc
                + jnp.einsum(
                    "bhqk,bkhd->bqhd", grad_scores, k_rows, preferred_element_type=jnp.float32
                )
                * inv_root
            )
            dk_part = (
                jnp.einsum(
                    "bhqk,bqhd->bkhd", grad_scores, q_rows, preferred_element_type=jnp.float32
                )
                * inv_root
            )
            dv_part = jnp.einsum(
                "bhqk,bqhd->bkhd",
                exp_scores.astype(jnp.bfloat16),
                g_rows,
                preferred_element_type=jnp.float32,
            )
            dk_slice = lax.dynamic_slice_in_dim(dk_all, k_start, k_block, 1) + dk_part
            dv_slice = lax.dynamic_slice_in_dim(dv_all, k_start, k_block, 1) + dv_part
            dk_all = lax.dynamic_update_slice_in_dim(dk_all, dk_slice, k_start, 1)
            dv_all = lax.dynamic_update_slice_in_dim(dv_all, dv_slice, k_start, 1)
            return (dq_acc, dk_all, dv_all)

        start_state = (jnp.zeros((seq_count, q_block, heads_here, HD), jnp.float32), grad_k, grad_v)
        dq_block, grad_k, grad_v = lax.fori_loop(
            0, (offset + q_block) // k_block, key_step, start_state
        )
        grad_q = lax.dynamic_update_slice_in_dim(grad_q, dq_block, offset, 1)
        return (grad_q, grad_k, grad_v)

    empty = jnp.zeros((seq_count, length, heads_here, HD), jnp.float32)
    grad_q, grad_k, grad_v = lax.fori_loop(0, length // q_block, query_step, (empty, empty, empty))
    cosine, sine_table = rope_tables(jnp.arange(length, dtype=jnp.int32), width_here)
    grad_q = grad_q.reshape(seq_count, length, width_here)
    grad_k = grad_k.reshape(seq_count, length, width_here)
    grad_v = grad_v.reshape(seq_count, length, width_here)
    raw_q = grad_q * cosine + rotate_back(grad_q * sine_table)
    raw_k = grad_k * cosine + rotate_back(grad_k * sine_table)
    return jnp.stack([raw_q, raw_k, grad_v]).astype(jnp.bfloat16)


def body(residual_in, attn_gain, mlp_gain, w_qkv, w_out, w_gate_up, w_down, cotangent):
    seq_count, shard_len, model_width = residual_in.shape
    tokens = seq_count * shard_len
    seq_index = lax.axis_index("seq")
    positions = seq_index * shard_len + jnp.arange(tokens, dtype=jnp.int32) % shard_len
    cosine, sine_table = rope_tables(positions, model_width)
    inputs = residual_in.reshape(tokens, model_width).astype(jnp.float32)
    gain_one = attn_gain.astype(jnp.float32)
    gain_two = mlp_gain.astype(jnp.float32)
    scale_one = rms_scale(inputs)
    normed_one = (inputs * scale_one * gain_one).astype(jnp.bfloat16)
    qkv_full, out_full = (
        lax.all_gather(w_qkv, "fsdp", axis=0, tiled=True),
        lax.all_gather(w_out, "fsdp", axis=0, tiled=True),
    )
    projected = jnp.einsum("td,fpd->ptf", normed_one, qkv_full, preferred_element_type=jnp.float32)
    queries = (projected[0] * cosine + rotate(projected[0]) * sine_table).astype(jnp.bfloat16)
    key_rows = (projected[1] * cosine + rotate(projected[1]) * sine_table).astype(jnp.bfloat16)
    values = projected[2].astype(jnp.bfloat16)
    stacked = jnp.stack([queries, key_rows, values]).reshape(3, seq_count, shard_len, model_width)
    head_view = lax.all_to_all(stacked, "seq", split_axis=3, concat_axis=2, tiled=True)
    attended, totals = attend_forward(head_view[0], head_view[1], head_view[2])
    attended_heads = attended.astype(jnp.bfloat16)
    sent_back = lax.all_to_all(attended_heads, "seq", split_axis=1, concat_axis=2, tiled=True)
    attended_low = sent_back.reshape(tokens, model_width)
    branch = jnp.einsum("ti,fi->tf", attended_low, out_full, preferred_element_type=jnp.float32)
    residual = inputs + branch
    scale_two = rms_scale(residual)
    normed_two = (residual * scale_two * gain_two).astype(jnp.bfloat16)
    up_full, down_full = (
        lax.all_gather(w_gate_up, "fsdp", axis=0, tiled=True),
        lax.all_gather(w_down, "fsdp", axis=0, tiled=True),
    )
    gate_up = jnp.einsum("td,jpd->ptj", normed_two, up_full, preferred_element_type=jnp.float32)
    hidden = (jax.nn.silu(gate_up[0]) * gate_up[1]).astype(jnp.bfloat16)
    mlp_term = jnp.einsum("tj,fj->tf", hidden, down_full, preferred_element_type=jnp.float32)
    layer_out = (
        (residual + mlp_term).astype(jnp.bfloat16).reshape(seq_count, shard_len, model_width)
    )
    grad_out = cotangent.reshape(tokens, model_width)
    up_again, down_again = (
        lax.all_gather(w_gate_up, "fsdp", axis=0, tiled=True),
        lax.all_gather(w_down, "fsdp", axis=0, tiled=True),
    )
    grad_hidden = jnp.einsum("tf,fj->tj", grad_out, down_again, preferred_element_type=jnp.float32)
    sigmoid_gate = jax.nn.sigmoid(gate_up[0])
    grad_gate = grad_hidden * gate_up[1] * sigmoid_gate * (1.0 + gate_up[0] * (1.0 - sigmoid_gate))
    grad_up = grad_hidden * jax.nn.silu(gate_up[0])
    grad_gu = jnp.stack([grad_gate, grad_up]).astype(jnp.bfloat16)
    grad_normed_two = jnp.einsum(
        "ptj,jpd->td", grad_gu, up_again, preferred_element_type=jnp.float32
    )
    ff_width = grad_gu.shape[2]
    unit_rows = jnp.concatenate([grad_gu, hidden[None]], axis=0).reshape(
        3, seq_count, shard_len, ff_width
    )
    unit_cols = lax.all_to_all(unit_rows, "seq", split_axis=3, concat_axis=2, tiled=True)
    normed_piece = lax.all_gather(
        normed_two.reshape(seq_count, shard_len, model_width), "seq", axis=1, tiled=True
    )
    grad_piece = lax.all_gather(cotangent, "seq", axis=1, tiled=True)
    gu_part = jnp.einsum(
        "psnj,snd->jpd", unit_cols[:2], normed_piece, preferred_element_type=jnp.float32
    )
    down_part = jnp.einsum(
        "snf,snj->fj", grad_piece, unit_cols[2], preferred_element_type=jnp.float32
    )
    gu_part, down_part = (gu_part, down_part)
    grad_gate_up, grad_down = (
        lax.psum_scatter(
            gu_part.astype(jnp.bfloat16), "fsdp", scatter_dimension=0, tiled=True
        ).astype(jnp.float32),
        lax.psum_scatter(
            down_part.astype(jnp.bfloat16), "fsdp", scatter_dimension=1, tiled=True
        ).astype(jnp.float32),
    )
    grad_norm_two, grad_gain_two = rms_back(grad_normed_two, residual, scale_two, gain_two)
    grad_residual = grad_out.astype(jnp.float32) + grad_norm_two
    qkv_back, out_back = (
        lax.all_gather(w_qkv, "fsdp", axis=0, tiled=True),
        lax.all_gather(w_out, "fsdp", axis=0, tiled=True),
    )
    grad_branch = grad_residual.astype(jnp.bfloat16)
    grad_attended = jnp.einsum(
        "tf,fi->ti", grad_branch, out_back, preferred_element_type=jnp.float32
    )
    grad_attended = grad_attended.astype(jnp.bfloat16).reshape(seq_count, shard_len, model_width)
    grad_heads = lax.all_to_all(grad_attended, "seq", split_axis=2, concat_axis=1, tiled=True)
    grad_stacked = attend_backward(
        head_view[0], head_view[1], head_view[2], attended, totals, grad_heads
    )
    normed_piece = lax.all_gather(
        normed_one.reshape(seq_count, shard_len, model_width), "seq", axis=1, tiled=True
    )
    branch_piece = lax.all_gather(
        grad_branch.reshape(seq_count, shard_len, model_width), "seq", axis=1, tiled=True
    )
    grad_piece = grad_stacked
    qkv_part = jnp.einsum(
        "psnf,snd->fpd", grad_piece, normed_piece, preferred_element_type=jnp.float32
    )
    out_part = jnp.einsum(
        "snf,sni->fi", branch_piece, attended_heads, preferred_element_type=jnp.float32
    )
    qkv_part, out_part = (qkv_part, out_part)
    grad_qkv, grad_out_proj = (
        lax.psum_scatter(
            qkv_part.astype(jnp.bfloat16), "fsdp", scatter_dimension=0, tiled=True
        ).astype(jnp.float32),
        lax.psum_scatter(
            out_part.astype(jnp.bfloat16), "fsdp", scatter_dimension=1, tiled=True
        ).astype(jnp.float32),
    )
    grad_projected = lax.all_to_all(grad_stacked, "seq", split_axis=2, concat_axis=3, tiled=True)
    grad_projected = grad_projected.reshape(3, tokens, model_width)
    grad_normed_one = jnp.einsum(
        "ptf,fpd->td", grad_projected, qkv_back, preferred_element_type=jnp.float32
    )
    grad_norm_one, grad_gain_one = rms_back(grad_normed_one, inputs, scale_one, gain_one)
    grad_input = (grad_residual + grad_norm_one).reshape(seq_count, shard_len, model_width)
    grad_attn_gain, grad_mlp_gain = (
        lax.psum_scatter(grad_gain_one, ("fsdp", "seq"), scatter_dimension=0, tiled=True),
        lax.psum_scatter(grad_gain_two, ("fsdp", "seq"), scatter_dimension=0, tiled=True),
    )
    return (
        layer_out,
        grad_input,
        grad_attn_gain,
        grad_mlp_gain,
        grad_qkv,
        grad_out_proj,
        grad_gate_up,
        grad_down,
    )


def solution(mesh):
    return jax.shard_map(
        body,
        mesh=mesh,
        in_specs=(
            P("fsdp", "seq", None),
            P(),
            P(),
            P("fsdp", None, None),
            P("fsdp", None),
            P("fsdp", None, None),
            P("fsdp", None),
            P("fsdp", "seq", None),
        ),
        out_specs=(
            P("fsdp", "seq", None),
            P("fsdp", "seq", None),
            P(("fsdp", "seq")),
            P(("fsdp", "seq")),
            P(("seq", "fsdp"), None, None),
            P(None, ("seq", "fsdp")),
            P(("seq", "fsdp"), None, None),
            P(None, ("seq", "fsdp")),
        ),
        check_vma=False,
    )
```

profile of v0, /device:TPU:0, one launch (start us, length us, event | category | flops | bytes accessed | tf_op | source)
XLA Modules:
  0.0 1827.8 jit_solution(5378411040820716253)
XLA Ops:
  8.7 18.1 copy.202
  28.7 211.5 %all-gather.11.cloned.1.call-done = bf16[2048,3,2048]{2,0,1:T(8,128)(2,1)} async-done(((bf16[512,3,2048]{2,0,1:T(8,128)(2,1)}), bf16[2048,3,2048]{2,0,1:T(8,128)(2,1)}) %all-gather.11.cloned.1.call-update) | async-done | bytes 25165840 | tf_op jit(solution)/shard_map/all_gather | solution.py:192
  240.2 13.5 convolution_bitcast_fusion.3
  284.0 49.0 %all-to-all-done = bf16[3,1,128,2048]{2,0,1,3:T(4,128)(2,1)S(1)} async-done(((bf16[3,1,128,2048]{2,0,1,3:T(4,128)(2,1)}), bf16[3,1,128,2048]{2,0,1,3:T(4,128)(2,1)S(1)}, u32[]{:S(2)}, u32[]{:S(2)}) %all-to-all-start) | async-done | bytes 1572896 | tf_op jit(solution)/shard_map/all_to_all | solution.py:200
  340.4 17.2 while.118
  347.3 10.2 while.121
  376.2 14.0 all-to-all-done.1
  395.3 6.5 multiply_reduce_fusion.3
  402.0 506.1 %all-gather.15.cloned.1.call-done = bf16[8192,2,2048]{2,0,1:T(8,128)(2,1)} async-done(((bf16[2048,2,2048]{2,0,1:T(8,128)(2,1)}), bf16[8192,2,2048]{2,0,1:T(8,128)(2,1)}) %all-gather.15.cloned.1.call-update) | async-done | bytes 67108880 | tf_op jit(solution)/shard_map/all_gather | solution.py:210
  908.1 37.6 %convolution_bitcast_fusion.2 = f32[2,128,8192]{2,1,0:T(8,128)} fusion(bf16[8192,2,2048]{2,0,1:T(8,128)(2,1)} %all-gather.15.cloned.1.call-done, bf16[128,2048]{1,0:T(8,128)(2,1)S(1)} %multiply_convert_fusion.2), kind=kOutput, calls=%fused_computation.67 | convolution fusion | flops 8589934592 | bytes 76021760 | tf_op jit(solution)/shard_map/td,jpd->ptj/dot_general | solution.py:213
  945.7 261.2 %all-gather.17.cloned.1.call-done = bf16[2048,8192]{1,0:T(8,128)(2,1)} async-done(((bf16[512,8192]{1,0:T(8,128)(2,1)}), bf16[2048,8192]{1,0:T(8,128)(2,1)}) %all-gather.17.cloned.1.call-update) | async-done | bytes 33554448 | tf_op jit(solution)/shard_map/all_gather | solution.py:211
  1206.9 19.1 %fusion.83 = (bf16[1,128,8192]{2,1,0:T(8,128)(2,1)}, bf16[1,128,8192]{2,1,0:T(8,128)(2,1)}) fusion(f32[2,128,8192]{2,1,0:T(8,128)} %convolution_bitcast_fusion.2, bf16[2048,8192]{1,0:T(8,128)(2,1)} %all-gather.17.cloned.1.call-done, bf16[1,128,2048]{2,1,0:T(8,128)(2,1)} %param.23), kind=kOutput, calls=%fused_computation.108 | convolution fusion | flops 4308598784 | bytes 46661632 | tf_op jit(solution)/shard_map/tf,fj->tj/dot_general | solution.py:224
  1226.0 25.3 %multiply_reduce_fusion = (f32[2048]{0:T(1024)}, f32[128]{0:T(128)S(1)}, f32[128,2048]{1,0:T(8,128)S(1)}) fusion(f32[128,2048]{1,0:T(8,128)S(1)} %get-tuple-element.716, f32[128]{0:T(128)S(1)} %get-tuple-element.714, f32[2048]{0:T(1024)S(1)} %convert_element_type.212, bf16[8192,2,2048]{2,0,1:T(8,128)(2,1)} %all-gather.15.cloned.1.call-done, ...), kind=kOutput, calls=%fused_computation.151 | convolution fusion | flops 8593602560 | bytes 73417728 | tf_op jit(solution)/shard_map/ptj,jpd->td/dot_general | solution.py:229
  1266.0 11.5 reduce.4
  1282.9 6.5 maximum_bitcast_fusion
  1289.4 13.2 copy.216
  1302.6 8.8 all-to-all-done.2
  1329.4 37.3 %while.120 = (s32[]{:T(128)}, f32[1,1024,4,64]{1,3,2,0:T(8,128)}, f32[1,1024,4,64]{1,3,2,0:T(8,128)S(1)}, f32[1,1024,4,64]{1,3,2,0:T(8,128)}, bf16[1,1024,4,64]{...) while((s32[]{:T(128)}, f32[1,1024,4,64]{1,3,2,0:T(8,128)}, ...), condition=%wide.region_12.13_spmd, body=%wide.region_9.12_spmd.sunk | while | flops 340329248 | bytes 17070880 | solution.py:170
  1331.2 10.7 while.122
  1344.5 21.4 %while.122 = (s32[]{:T(128)}, f32[1,512,4,64]{1,3,2,0:T(8,128)S(1)}, f32[1,1024,4,64]{1,3,2,0:T(8,128)S(1)}, f32[1,1024,4,64]{1,3,2,0:T(8,128)}, s32[]{:T(128)},...) while((s32[]{:T(128)}, f32[1,512,4,64]{1,3,2,0:T(8,128)S(1)}, ...), condition=%wide.region_11.11_spmd.clone, body=%wide.region_10.10_spmd.clone.sunk | while | flops 340329216 | bytes 14432507 | solution.py:163
  1390.2 7.5 fusion.72
  1397.7 7.8 copy.215
  1410.0 157.5 %all-to-all-done.4 = bf16[3,1,128,8192]{2,0,1,3:T(4,128)(2,1)} async-done(((bf16[3,1,128,8192]{2,0,1,3:T(4,128)(2,1)}), bf16[3,1,128,8192]{2,0,1,3:T(4,128)(2,1)}, u32[]{:S(2)}, u32[]{:S(2)}) %all-to-all-start.4) | async-done | bytes 6291488 | tf_op jit(solution)/shard_map/all_to_all | solution.py:236
  1577.6 9.5 convert_bitcast_fusion.1
  1591.7 6.3 copy.218
  1598.0 14.1 convert_bitcast_fusion
  1621.3 19.0 %fusion.80 = bf16[1,128,2048]{2,1,0:T(8,128)(2,1)} fusion(f32[128,2048]{1,0:T(8,128)S(1)} %copy-done.5, bf16[2048,8192]{1,0:T(8,128)(2,1)} %all-gather.17.cloned.1.call-done, f32[2,128,8192]{2,1,0:T(8,128)} %convolution_bitcast_fusion.2), kind=kOutput, calls=%fused_computation.106 | convolution fusion | flops 4301783040 | bytes 43515904 | tf_op jit(solution)/shard_map/tj,fj->tf/dot_general | solution.py:215
  1640.2 28.7 %all-to-all-done.3 = bf16[3,1,1024,256]{3,0,1,2:T(4,128)(2,1)S(1)} async-done(((bf16[3,1,1024,256]{3,0,1,2:T(4,128)(2,1)}), bf16[3,1,1024,256]{3,0,1,2:T(4,128)(2,1)S(1)}, u32[]{:S(2)}, u32[]{:S(2)}) %all-to-all-start.3) | async-done | bytes 1572896 | tf_op jit(solution)/shard_map/all_to_all | solution.py:293
  1673.8 13.6 fusion.107
  1687.4 38.0 %all-reduce.3 = (f32[2048]{0:T(1024)S(1)}, f32[2048]{0:T(1024)S(1)}) all-reduce(f32[2048]{0:T(1024)S(1)} %get-tuple-element.610, f32[2048]{0:T(1024)S(1)} %copy-done.22), channel_id=4, replica_groups=mesh['fsdp'=4,'seq'=8] {'fsdp','seq'}, use_global_device_ids=true, to_apply=%region_15.16.clone | all-reduce | flops 4096 | bytes 32768
  1737.1 77.2 %reduce-scatter.6.cloned.1.call-done = bf16[256,2,2048]{0,2,1:T(8,128)(2,1)} async-done(((bf16[1024,2,2048]{0,2,1:T(8,128)(2,1)}), bf16[256,2,2048]{0,2,1:T(8,128)(2,1)}) %reduce-scatter.6.cloned.1.call-update) | async-done | bytes 2097168 | tf_op jit(solution)/shard_map/reduce_scatter | solution.py:249
  1814.3 6.4 copy.222
  (296 shorter events, 228.9 us)
Async XLA Ops:
  7.2 233.0 %all-gather.11.cloned.1.call-start = ((), (), s32[]{:S(2)}) async-start(), calls=%async_computation.8 | async-start | bytes 31457280 | tf_op jit(solution)/shard_map/all_gather | solution.py:192
  7.9 387.4 %all-gather.13.cloned.1.call-start = ((), (), s32[]{:S(2)}) async-start(), calls=%async_computation.9 | async-start | bytes 10485760 | tf_op jit(solution)/shard_map/all_gather | solution.py:193
  8.7 899.4 %all-gather.15.cloned.1.call-start = ((), (), s32[]{:S(2)}) async-start(), calls=%async_computation.10 | async-start | bytes 83886080 | tf_op jit(solution)/shard_map/all_gather | solution.py:210
  26.8 1180.0 %all-gather.17.cloned.1.call-start = ((), (), s32[]{:S(2)}) async-start(), calls=%async_computation.11 | async-start | bytes 41943040 | tf_op jit(solution)/shard_map/all_gather | solution.py:211
  27.5 347.3 %copy-start.20 = (f32[2048]{0:T(1024)}, f32[2048]{0:T(1024)S(1)}, u32[]{:S(2)}) copy-start(f32[2048]{0:T(1024)S(1)} %convert_element_type.204) | copy-start | bytes 24580
  28.7 346.2 %copy-start.23 = (f32[128]{0:T(128)}, f32[128]{0:T(128)S(1)}, u32[]{:S(2)}) copy-start(f32[128]{0:T(128)S(1)} %get-tuple-element.712) | copy-start | bytes 1540
  278.9 54.1 %all-to-all-start = ((bf16[3,1,128,2048]{2,0,1,3:T(4,128)(2,1)}), bf16[3,1,128,2048]{2,0,1,3:T(4,128)(2,1)S(1)}, u32[]{:S(2)}, u32[]{:S(2)}) async-start(bf16[3,1,128,2048]{2,0,1,3:T(4,128)(2,1)} %copy.196), calls=%async_computation | async-start | bytes 4194304 | tf_op jit(solution)/shard_map/all_to_all | solution.py:200
  357.6 18.3 %copy-start.7 = (f32[1,1024,4,64]{1,3,2,0:T(8,128)}, f32[1,1024,4,64]{1,3,2,0:T(8,128)S(1)}, u32[]{:S(2)}) copy-start(f32[1,1024,4,64]{1,3,2,0:T(8,128)S(1)} %get-tuple-element.501) | copy-start | bytes 3145732
  357.6 17.3 copy-start.2
  357.6 18.5 %copy-start.26 = (bf16[2048]{0:T(1024)(128)(2,1)S(1)}, bf16[2048]{0:T(1024)(128)(2,1)}, u32[]{:S(2)}) copy-start(bf16[2048]{0:T(1024)(128)(2,1)} %param.18) | copy-start | bytes 12292
  370.7 19.5 %all-to-all-start.1 = ((bf16[8,2,16384]{2,1,0:T(2,128)(2,1)}), bf16[8,2,16384]{2,1,0:T(2,128)(2,1)}, u32[]{:S(2)}, u32[]{:S(2)}) async-start(bf16[8,2,16384]{2,1,0:T(2,128)(2,1)} %reshape.879), calls=%async_computation.1 | async-start | bytes 1048576 | tf_op jit(solution)/shard_map/all_to_all | solution.py:203
  374.8 1015.3 %all-gather.19.cloned.1.call-start = ((), (), s32[]{:S(2)}) async-start(), calls=%async_computation.12 | async-start | bytes 4718592 | tf_op jit(solution)/shard_map/all_gather | solution.py:271
  375.9 1029.6 %all-gather.23.cloned.1.call-start = ((), (), s32[]{:S(2)}) async-start(), calls=%async_computation.17 | async-start | bytes 4718592 | tf_op jit(solution)/shard_map/all_gather | solution.py:274
  401.8 849.5 %copy-start.4 = (f32[128,2048]{1,0:T(8,128)}, f32[128,2048]{1,0:T(8,128)S(1)}, u32[]{:S(2)}) copy-start(f32[128,2048]{1,0:T(8,128)S(1)} %get-tuple-element.716) | copy-start | bytes 3145732
  402.0 543.7 %copy-start.11 = (bf16[128,2048]{1,0:T(8,128)(2,1)}, bf16[128,2048]{1,0:T(8,128)(2,1)S(1)}, u32[]{:S(2)}) copy-start(bf16[128,2048]{1,0:T(8,128)(2,1)S(1)} %multiply_convert_fusion.2) | copy-start | bytes 1572868
  1226.0 25.4 %copy-start.16 = (bf16[1,128,2048]{2,1,0:T(8,128)(2,1)S(1)}, bf16[1,128,2048]{2,1,0:T(8,128)(2,1)}, u32[]{:S(2)}) copy-start(bf16[1,128,2048]{2,1,0:T(8,128)(2,1)} %param.23) | copy-start | bytes 1572868
  1252.9 324.7 %all-gather.21.cloned.1.call-start = ((), (), s32[]{:S(2)}) async-start(), calls=%async_computation.15 | async-start | bytes 4718592 | tf_op jit(solution)/shard_map/all_gather | solution.py:240
  1253.6 344.4 %all-gather.25.cloned.1.call-start = ((), (), s32[]{:S(2)}) async-start(), calls=%async_computation.18 | async-start | bytes 4718592 | tf_op jit(solution)/shard_map/all_gather | solution.py:237
  1278.4 32.9 %all-to-all-start.2 = ((bf16[8,2,16384]{2,1,0:T(2,128)(2,1)}), bf16[8,2,16384]{2,1,0:T(2,128)(2,1)S(1)}, u32[]{:S(2)}, u32[]{:S(2)}) async-start(bf16[8,2,16384]{2,1,0:T(2,128)(2,1)} %reshape.881), calls=%async_computation.2 | async-start | bytes 1048576 | tf_op jit(solution)/shard_map/all_to_all | solution.py:267
  1311.3 256.2 %all-to-all-start.4 = ((bf16[3,1,128,8192]{2,0,1,3:T(4,128)(2,1)}), bf16[3,1,128,8192]{2,0,1,3:T(4,128)(2,1)}, u32[]{:S(2)}, u32[]{:S(2)}) async-start(bf16[3,1,128,8192]{2,0,1,3:T(4,128)(2,1)} %copy.216), calls=%async_computation.5 | async-start | bytes 16777216 | tf_op jit(solution)/shard_map/all_to_all | solution.py:236
  1316.2 8.6 copy-start.8
  1316.3 413.0 %all-reduce.6.cloned.1.call-start = ((), (), s32[]{:S(2)}) async-start(), calls=%async_computation.19 | async-start | bytes 8388608
  1405.5 327.3 %reduce-scatter.4.cloned.1.call-start = ((), (), s32[]{:S(2)}) async-start(), calls=%async_computation.13 | async-start | bytes 1310720 | tf_op jit(solution)/shard_map/reduce_scatter | solution.py:289
  1410.0 324.5 %reduce-scatter.8.cloned.1.call-start = ((), (), s32[]{:S(2)}) async-start(), calls=%async_computation.16 | async-start | bytes 5242880 | tf_op jit(solution)/shard_map/reduce_scatter | solution.py:252
  1587.1 227.2 %reduce-scatter.6.cloned.1.call-start = ((), (), s32[]{:S(2)}) async-start(), calls=%async_computation.14 | async-start | bytes 10485760 | tf_op jit(solution)/shard_map/reduce_scatter | solution.py:249
  1616.2 52.8 %all-to-all-start.3 = ((bf16[3,1,1024,256]{3,0,1,2:T(4,128)(2,1)}), bf16[3,1,1024,256]{3,0,1,2:T(4,128)(2,1)S(1)}, u32[]{:S(2)}, u32[]{:S(2)}) async-start(bf16[3,1,1024,256]{3,0,1,2:T(4,128)(2,1)} %copy.210), calls=%async_computation.3 | async-start | bytes 4194304 | tf_op jit(solution)/shard_map/all_to_all | solution.py:293
  1640.2 33.6 %copy-start.3 = (bf16[1,128,2048]{2,1,0:T(8,128)(2,1)S(1)}, bf16[1,128,2048]{2,1,0:T(8,128)(2,1)}, u32[]{:S(2)}) copy-start(bf16[1,128,2048]{2,1,0:T(8,128)(2,1)} %param.16) | copy-start | bytes 1572868
  1640.2 33.6 %copy-start.21 = (f32[2048]{0:T(1024)S(1)}, f32[2048]{0:T(1024)}, u32[]{:S(2)}) copy-start(f32[2048]{0:T(1024)} %copy-done.20) | copy-start | bytes 24580
  1640.2 33.6 %copy-start.24 = (f32[128]{0:T(128)S(1)}, f32[128]{0:T(128)}, u32[]{:S(2)}) copy-start(f32[128]{0:T(128)} %copy-done.23) | copy-start | bytes 1540
  1673.8 13.6 copy-start.22
  1673.8 52.8 %copy-start.12 = (f32[128,2048]{1,0:T(8,128)S(1)}, f32[128,2048]{1,0:T(8,128)}, u32[]{:S(2)}) copy-start(f32[128,2048]{1,0:T(8,128)} %get-tuple-element.683) | copy-start | bytes 3145732
  1673.8 52.8 %copy-start.27 = (f32[128]{0:T(128)S(1)}, f32[128]{0:T(128)}, u32[]{:S(2)}) copy-start(f32[128]{0:T(128)} %get-tuple-element.711) | copy-start | bytes 1540
  (19 other events, 76.8 us)
Sparse Core Ops, SparseCore 0:
  9.8 230.2 all-gather.10
  242.0 87.4 all-gather.12
  331.4 576.6 all-gather.14
  909.8 297.0 all-gather.16
  1208.3 46.8 all-gather.18
  1257.3 56.8 all-gather.22
  1315.8 78.7 all-gather.20
  1396.2 135.9 all-gather.24
  1536.0 101.4 all-reduce.5
  1640.3 27.9 reduce-scatter.3
  1671.2 53.6 reduce-scatter.7
  1727.8 86.4 reduce-scatter.5
where the time goes:
time: 1840 us; the launch traced here: 1830 us
  waiting for transfers between devices  1320 us (72%)
  matrix products  220 us (12%)
  local copies, waits for them, and re-layouts  140 us (8%)
  other arithmetic  72.3 us (4%)
  blocking collectives  38 us (2%)
  starting transfers between devices  23.7 us (1%)
    all_gather x1, waiting for transfers between devices, body(): lax.all_gather(w_gate_up, 'fsdp', axis=0, tiled=True)  506 us
    all_gather x1, waiting for transfers between devices, body(): lax.all_gather(w_down, 'fsdp', axis=0, tiled=True)  261 us
    all_gather x1, waiting for transfers between devices, body(): lax.all_gather(w_qkv, 'fsdp', axis=0, tiled=True)  211 us
    all_to_all x1, waiting for transfers between devices, body(): lax.all_to_all(unit_rows, 'seq', split_axis=3, concat_axis=2, tiled=True)  157 us
    reduce_scatter x1, waiting for transfers between devices, body(): lax.psum_scatter(gu_part.astype(jnp.bfloat16), 'fsdp', scatter_dimension=...  77.2 us
    all_to_all x1, waiting for transfers between devices, body(): lax.all_to_all(stacked, 'seq', split_axis=3, concat_axis=2, tiled=True)  49 us
    unnamed x69, local copies, waits for them, and re-layouts  43.5 us
    unnamed x1, blocking collectives  38 us
  transfers between devices with their start and end apart: 17, of which 9 were waited for; matrix products, arithmetic and copies ran while one was open for 23% of the time, Pallas kernels for 0%

commit v1 on v0

--- a/solution.py
+++ b/solution.py
@@ -7,6 +7,24 @@
 HD = 64
 NORM_EPS = 1e-05
 ROPE_BASE = 130000.0
+
+
+def collect(value, axis, dim):
+    ways, here, step = (lax.axis_size(axis), lax.axis_index(axis), value.shape[dim])
+    lengths = [n * ways if d == dim else n for d, n in enumerate(value.shape)]
+    full = lax.dynamic_update_slice_in_dim(
+        jnp.zeros(lengths, value.dtype), value, here * step, axis=dim
+    )
+    going_up = going_down = value
+    for far in range(1, ways // 2 + 1):
+        going_up = lax.ppermute(going_up, axis, [(d, (d + 1) % ways) for d in range(ways)])
+        full = lax.dynamic_update_slice_in_dim(full, going_up, (here - far) % ways * step, axis=dim)
+        if 2 * far < ways:
+            going_down = lax.ppermute(going_down, axis, [(d, (d - 1) % ways) for d in range(ways)])
+            full = lax.dynamic_update_slice_in_dim(
+                full, going_down, (here + far) % ways * step, axis=dim
+            )
+    return full
 
 
 def rotate(matrix):
@@ -208,7 +226,7 @@
     normed_two = (residual * scale_two * gain_two).astype(jnp.bfloat16)
     up_full, down_full = (
         lax.all_gather(w_gate_up, "fsdp", axis=0, tiled=True),
-        lax.all_gather(w_down, "fsdp", axis=0, tiled=True),
+        collect(w_down, "fsdp", 0),
     )
     gate_up = jnp.einsum("td,jpd->ptj", normed_two, up_full, preferred_element_type=jnp.float32)
     hidden = (jax.nn.silu(gate_up[0]) * gate_up[1]).astype(jnp.bfloat16)

time: 1840 us -> 2390 us (1.30)
  waiting for transfers between devices: 1320 us -> 1830 us
  local copies, waits for them, and re-layouts: 140 us -> 179 us
    ppermute x0 -> x3, waiting for transfers between devices: none -> 613 us  [the longest x2 432 us: collect(): lax.ppermute(going_up, axis, [(d, (d + 1) % ways) for d in range(ways)])]
    reduce_scatter x1, waiting for transfers between devices: 77.2 us -> 0.01 us  [body(): lax.psum_scatter(gu_part.astype(jnp.bfloat16), 'fsdp', scatter_dimension=...]
    dynamic_update_slice x0 -> x4, local copies, waits for them, and re-layouts: none -> 31.4 us  [the longest x2 16 us: collect(): lax.dynamic_update_slice_in_dim(full, going_up, (here - far) % ways * ste...]
    all_to_all x1, waiting for transfers between devices: 28.7 us -> 0.01 us  [body(): lax.all_to_all(grad_stacked, 'seq', split_axis=2, concat_axis=3, tiled=True)]
  transfers between devices with their start and end apart: 17 -> 20, of which waited for: 9 -> 10; matrix products, arithmetic and copies ran while one was open for 23% -> 19% of each run, Pallas kernels for 0% -> 0%
where the time goes in v1:
time: 2390 us; the launch traced here: 2380 us
  waiting for transfers between devices  1830 us (77%)
  matrix products  218 us (9%)
  local copies, waits for them, and re-layouts  179 us (7%)
  other arithmetic  70.7 us (3%)
  blocking collectives  37.4 us (2%)
  starting transfers between devices  27.6 us (1%)
    all_gather x1, waiting for transfers between devices, body(): lax.all_gather(w_gate_up, 'fsdp', axis=0, tiled=True)  507 us
    ppermute x2, waiting for transfers between devices, collect(): lax.ppermute(going_up, axis, [(d, (d + 1) % ways) for d in range(ways)])  432 us
    all_gather x1, waiting for transfers between devices, body(): lax.all_gather(w_down, 'fsdp', axis=0, tiled=True)  261 us
    all_gather x1, waiting for transfers between devices, body(): lax.all_gather(w_qkv, 'fsdp', axis=0, tiled=True)  211 us
    ppermute x1, waiting for transfers between devices, collect(): lax.ppermute(going_down, axis, [(d, (d - 1) % ways) for d in range(ways)])  181 us
    all_to_all x1, waiting for transfers between devices, body(): lax.all_to_all(unit_rows, 'seq', split_axis=3, concat_axis=2, tiled=True)  162 us
    all_to_all x1, waiting for transfers between devices, body(): lax.all_to_all(stacked, 'seq', split_axis=3, concat_axis=2, tiled=True)  49 us
  transfers between devices with their start and end apart: 20, of which 10 were waited for; matrix products, arithmetic and copies ran while one was open for 19% of the time, Pallas kernels for 0%

profile of v1, /device:TPU:0, one launch (start us, length us, event | category | flops | bytes accessed | tf_op | source)
XLA Modules:
  0.0 2379.1 jit_solution(9604766458613132319)
XLA Ops:
  8.7 18.1 copy.202
  28.7 211.5 %all-gather.11.cloned.1.call-done = bf16[2048,3,2048]{2,0,1:T(8,128)(2,1)} async-done(((bf16[512,3,2048]{2,0,1:T(8,128)(2,1)}), bf16[2048,3,2048]{2,0,1:T(8,128)(2,1)}) %all-gather.11.cloned.1.call-update) | async-done | bytes 25165840 | tf_op jit(solution)/shard_map/all_gather | solution.py:210
  240.2 13.5 convolution_bitcast_fusion.3
  283.7 49.0 %all-to-all-done = bf16[3,1,128,2048]{2,0,1,3:T(4,128)(2,1)S(1)} async-done(((bf16[3,1,128,2048]{2,0,1,3:T(4,128)(2,1)}), bf16[3,1,128,2048]{2,0,1,3:T(4,128)(2,1)S(1)}, u32[]{:S(2)}, u32[]{:S(2)}) %all-to-all-start) | async-done | bytes 1572896 | tf_op jit(solution)/shard_map/all_to_all | solution.py:218
  340.0 16.9 while.118
  346.8 10.0 while.121
  375.6 13.9 all-to-all-done.1
  401.4 506.7 %all-gather.15.cloned.1.call-done = bf16[8192,2,2048]{2,0,1:T(8,128)(2,1)} async-done(((bf16[2048,2,2048]{2,0,1:T(8,128)(2,1)}), bf16[8192,2,2048]{2,0,1:T(8,128)(2,1)}) %all-gather.15.cloned.1.call-update) | async-done | bytes 67108880 | tf_op jit(solution)/shard_map/all_gather | solution.py:228
  908.1 37.6 %convolution_bitcast_fusion.2 = f32[2,128,8192]{2,1,0:T(8,128)} fusion(bf16[8192,2,2048]{2,0,1:T(8,128)(2,1)} %all-gather.15.cloned.1.call-done, bf16[128,2048]{1,0:T(8,128)(2,1)S(1)} %multiply_convert_fusion.2), kind=kOutput, calls=%fused_computation.67 | convolution fusion | flops 8589934592 | bytes 76021760 | tf_op jit(solution)/shard_map/td,jpd->ptj/dot_general | solution.py:231
  945.7 261.2 %all-gather.17.cloned.1.call-done = bf16[2048,8192]{1,0:T(8,128)(2,1)} async-done(((bf16[512,8192]{1,0:T(8,128)(2,1)}), bf16[2048,8192]{1,0:T(8,128)(2,1)}) %all-gather.17.cloned.1.call-update) | async-done | bytes 33554448 | tf_op jit(solution)/shard_map/all_gather | solution.py:240
  1206.9 19.1 fusion.83
  1226.0 25.3 %multiply_reduce_fusion = (f32[2048]{0:T(1024)}, f32[128]{0:T(128)S(1)}, f32[128,2048]{1,0:T(8,128)S(1)}) fusion(f32[128,2048]{1,0:T(8,128)S(1)} %get-tuple-element.716, f32[128]{0:T(128)S(1)} %get-tuple-element.714, f32[2048]{0:T(1024)S(1)} %convert_element_type.212, bf16[8192,2,2048]{2,0,1:T(8,128)(2,1)} %all-gather.15.cloned.1.call-done, ...), kind=kOutput, calls=%fused_computation.151 | convolution fusion | flops 8593602560 | bytes 73417728 | tf_op jit(solution)/shard_map/ptj,jpd->td/dot_general | solution.py:247
  1266.0 11.5 reduce.4
  1289.5 13.2 copy.216
  1302.7 8.6 all-to-all-done.2
  1329.0 37.3 %while.120 = (s32[]{:T(128)}, f32[1,1024,4,64]{1,3,2,0:T(8,128)}, f32[1,1024,4,64]{1,3,2,0:T(8,128)S(1)}, f32[1,1024,4,64]{1,3,2,0:T(8,128)}, bf16[1,1024,4,64]{...) while((s32[]{:T(128)}, f32[1,1024,4,64]{1,3,2,0:T(8,128)}, ...), condition=%wide.region_12.13_spmd, body=%wide.region_9.12_spmd.sunk | while | flops 340329248 | bytes 17070864 | solution.py:188
  1330.7 10.7 while.122
  1344.1 21.4 while.122
  1393.1 7.8 copy.215
  1405.6 161.9 %all-to-all-done.4 = bf16[3,1,128,8192]{2,0,1,3:T(4,128)(2,1)} async-done(((bf16[3,1,128,8192]{2,0,1,3:T(4,128)(2,1)}), bf16[3,1,128,8192]{2,0,1,3:T(4,128)(2,1)}, u32[]{:S(2)}, u32[]{:S(2)}) %all-to-all-start.4) | async-done | bytes 6291488 | tf_op jit(solution)/shard_map/all_to_all | solution.py:254
  1577.5 9.4 convert_bitcast_fusion.1
  1599.5 14.1 convert_bitcast_fusion
  1615.5 268.1 %collective-permute-done = bf16[512,8192]{1,0:T(8,128)(2,1)} collective-permute-done((bf16[512,8192]{1,0:T(8,128)(2,1)}, bf16[512,8192]{1,0:T(8,128)(2,1)}, u32[]{:S(2)}, u32[]{:S(2)}) %collective-permute-start) | collective-permute-done | bytes 8388640 | tf_op jit(solution)/shard_map/ppermute | solution.py:20
  1886.0 11.1 broadcast_in_dim.24
  1897.1 7.7 constant_dynamic-update-slice_fusion.5
  1904.8 8.3 constant_dynamic-update-slice_fusion.4
  1913.1 181.2 %collective-permute-done.1 = bf16[512,8192]{1,0:T(8,128)(2,1)} collective-permute-done((bf16[512,8192]{1,0:T(8,128)(2,1)}, bf16[512,8192]{1,0:T(8,128)(2,1)}, u32[]{:S(2)}, u32[]{:S(2)}) %collective-permute-start.1) | collective-permute-done | bytes 8388640 | tf_op jit(solution)/shard_map/ppermute | solution.py:23
  2108.8 163.8 %collective-permute-done.2 = bf16[512,8192]{1,0:T(8,128)(2,1)} collective-permute-done((bf16[512,8192]{1,0:T(8,128)(2,1)}, bf16[512,8192]{1,0:T(8,128)(2,1)}, u32[]{:S(2)}, u32[]{:S(2)}) %collective-permute-start.2) | collective-permute-done | bytes 8388640 | tf_op jit(solution)/shard_map/ppermute | solution.py:20
  2272.7 7.7 constant_dynamic-update-slice_fusion.2
  2280.4 18.5 fusion.80
  2303.8 12.9 fusion.107
  2316.6 37.4 %all-reduce.3 = (f32[2048]{0:T(1024)S(1)}, f32[2048]{0:T(1024)S(1)}) all-reduce(f32[2048]{0:T(1024)S(1)} %get-tuple-element.610, f32[2048]{0:T(1024)S(1)} %copy-done.22), channel_id=4, replica_groups=mesh['fsdp'=4,'seq'=8] {'fsdp','seq'}, use_global_device_ids=true, to_apply=%region_15.16.clone | all-reduce | flops 4096 | bytes 32768
  (307 shorter events, 268.3 us)
Async XLA Ops:
  7.2 233.0 %all-gather.11.cloned.1.call-start = ((), (), s32[]{:S(2)}) async-start(), calls=%async_computation.8 | async-start | bytes 31457280 | tf_op jit(solution)/shard_map/all_gather | solution.py:210
  7.9 386.7 %all-gather.13.cloned.1.call-start = ((), (), s32[]{:S(2)}) async-start(), calls=%async_computation.9 | async-start | bytes 10485760 | tf_op jit(solution)/shard_map/all_gather | solution.py:211
  8.7 899.4 %all-gather.15.cloned.1.call-start = ((), (), s32[]{:S(2)}) async-start(), calls=%async_computation.10 | async-start | bytes 83886080 | tf_op jit(solution)/shard_map/all_gather | solution.py:228
  26.8 1180.0 %all-gather.17.cloned.1.call-start = ((), (), s32[]{:S(2)}) async-start(), calls=%async_computation.11 | async-start | bytes 41943040 | tf_op jit(solution)/shard_map/all_gather | solution.py:240
  27.5 346.7 %copy-start.20 = (f32[2048]{0:T(1024)}, f32[2048]{0:T(1024)S(1)}, u32[]{:S(2)}) copy-start(f32[2048]{0:T(1024)S(1)} %convert_element_type.204) | copy-start | bytes 24580
  28.7 345.5 %copy-start.23 = (f32[128]{0:T(128)}, f32[128]{0:T(128)S(1)}, u32[]{:S(2)}) copy-start(f32[128]{0:T(128)S(1)} %get-tuple-element.712) | copy-start | bytes 1540
  278.9 53.8 %all-to-all-start = ((bf16[3,1,128,2048]{2,0,1,3:T(4,128)(2,1)}), bf16[3,1,128,2048]{2,0,1,3:T(4,128)(2,1)S(1)}, u32[]{:S(2)}, u32[]{:S(2)}) async-start(bf16[3,1,128,2048]{2,0,1,3:T(4,128)(2,1)} %copy.196), calls=%async_computation | async-start | bytes 4194304 | tf_op jit(solution)/shard_map/all_to_all | solution.py:218
  357.0 18.3 copy-start.7
  357.0 18.5 copy-start.26
  370.0 19.5 all-to-all-start.1
  374.2 1011.4 %all-gather.19.cloned.1.call-start = ((), (), s32[]{:S(2)}) async-start(), calls=%async_computation.12 | async-start | bytes 4718592 | tf_op jit(solution)/shard_map/all_gather | solution.py:289
  375.3 1025.7 %all-gather.23.cloned.1.call-start = ((), (), s32[]{:S(2)}) async-start(), calls=%async_computation.17 | async-start | bytes 4718592 | tf_op jit(solution)/shard_map/all_gather | solution.py:292
  401.2 850.1 %copy-start.4 = (f32[128,2048]{1,0:T(8,128)}, f32[128,2048]{1,0:T(8,128)S(1)}, u32[]{:S(2)}) copy-start(f32[128,2048]{1,0:T(8,128)S(1)} %get-tuple-element.716) | copy-start | bytes 3145732
  401.4 544.3 %copy-start.11 = (bf16[128,2048]{1,0:T(8,128)(2,1)}, bf16[128,2048]{1,0:T(8,128)(2,1)S(1)}, u32[]{:S(2)}) copy-start(bf16[128,2048]{1,0:T(8,128)(2,1)S(1)} %multiply_convert_fusion.2) | copy-start | bytes 1572868
  1226.0 25.3 %copy-start.16 = (bf16[1,128,2048]{2,1,0:T(8,128)(2,1)S(1)}, bf16[1,128,2048]{2,1,0:T(8,128)(2,1)}, u32[]{:S(2)}) copy-start(bf16[1,128,2048]{2,1,0:T(8,128)(2,1)} %param.23) | copy-start | bytes 1572868
  1252.9 324.7 %all-gather.21.cloned.1.call-start = ((), (), s32[]{:S(2)}) async-start(), calls=%async_computation.15 | async-start | bytes 4718592 | tf_op jit(solution)/shard_map/all_gather | solution.py:258
  1253.6 345.9 %all-gather.25.cloned.1.call-start = ((), (), s32[]{:S(2)}) async-start(), calls=%async_computation.18 | async-start | bytes 4718592 | tf_op jit(solution)/shard_map/all_gather | solution.py:255
  1278.4 32.9 %all-to-all-start.2 = ((bf16[8,2,16384]{2,1,0:T(2,128)(2,1)}), bf16[8,2,16384]{2,1,0:T(2,128)(2,1)S(1)}, u32[]{:S(2)}, u32[]{:S(2)}) async-start(bf16[8,2,16384]{2,1,0:T(2,128)(2,1)} %reshape.881), calls=%async_computation.2 | async-start | bytes 1048576 | tf_op jit(solution)/shard_map/all_to_all | solution.py:285
  1311.3 256.2 %all-to-all-start.4 = ((bf16[3,1,128,8192]{2,0,1,3:T(4,128)(2,1)}), bf16[3,1,128,8192]{2,0,1,3:T(4,128)(2,1)}, u32[]{:S(2)}, u32[]{:S(2)}) async-start(bf16[3,1,128,8192]{2,0,1,3:T(4,128)(2,1)} %copy.216), calls=%async_computation.5 | async-start | bytes 16777216 | tf_op jit(solution)/shard_map/all_to_all | solution.py:254
  1316.3 1041.6 %all-reduce.6.cloned.1.call-start = ((), (), s32[]{:S(2)}) async-start(), calls=%async_computation.19 | async-start | bytes 8388608
  1401.0 960.4 %reduce-scatter.4.cloned.1.call-start = ((), (), s32[]{:S(2)}) async-start(), calls=%async_computation.13 | async-start | bytes 1310720 | tf_op jit(solution)/shard_map/reduce_scatter | solution.py:307
  1405.6 957.5 %reduce-scatter.8.cloned.1.call-start = ((), (), s32[]{:S(2)}) async-start(), calls=%async_computation.16 | async-start | bytes 5242880 | tf_op jit(solution)/shard_map/reduce_scatter | solution.py:270
  1587.0 778.7 %reduce-scatter.6.cloned.1.call-start = ((), (), s32[]{:S(2)}) async-start(), calls=%async_computation.14 | async-start | bytes 10485760 | tf_op jit(solution)/shard_map/reduce_scatter | solution.py:267
  1587.0 296.6 %collective-permute-start = (bf16[512,8192]{1,0:T(8,128)(2,1)}, bf16[512,8192]{1,0:T(8,128)(2,1)}, u32[]{:S(2)}, u32[]{:S(2)}) collective-permute-start(bf16[512,8192]{1,0:T(8,128)(2,1)} %param.22), channel_id=1, source_target_pairs={{0,8},{8,16},{16,24},{24,0},{1,9},{9,17},{17,25},{25,1},{2,10},{10... | collective-permute-start | bytes 25165832 | tf_op jit(solution)/shard_map/ppermute | solution.py:20
  1613.6 271.2 %copy-start.28 = (u32[32]{0:T(128)S(1)}, u32[32]{0:T(128)}, u32[]{:S(2)}) copy-start(u32[32]{0:T(128)} %constant.327) | copy-start | bytes 388
  1613.6 480.7 %collective-permute-start.1 = (bf16[512,8192]{1,0:T(8,128)(2,1)}, bf16[512,8192]{1,0:T(8,128)(2,1)}, u32[]{:S(2)}, u32[]{:S(2)}) collective-permute-start(bf16[512,8192]{1,0:T(8,128)(2,1)} %param.22), channel_id=1, source_target_pairs={{0,24},{8,0},{16,8},{24,16},{1,25},{9,1},{17,9},{25,17},{2,26},{10... | collective-permute-start | bytes 25165832 | tf_op jit(solution)/shard_map/ppermute | solution.py:23
  1883.6 389.1 %collective-permute-start.2 = (bf16[512,8192]{1,0:T(8,128)(2,1)}, bf16[512,8192]{1,0:T(8,128)(2,1)}, u32[]{:S(2)}, u32[]{:S(2)}) collective-permute-start(bf16[512,8192]{1,0:T(8,128)(2,1)} %collective-permute-done), channel_id=1, source_target_pairs={{0,8},{8,16},{16,24},{24,0},{1,9},{9,17},{17,25},{25,1},{2,10},{10... | collective-permute-start | bytes 25165832 | tf_op jit(solution)/shard_map/ppermute | solution.py:20
  1913.1 189.1 %copy-start.18 = (bf16[1,1024,256]{2,1,0:T(8,128)(2,1)S(1)}, bf16[1,1024,256]{2,1,0:T(8,128)(2,1)}, u32[]{:S(2)}) copy-start(bf16[1,1024,256]{2,1,0:T(8,128)(2,1)} %copy-done.17) | copy-start | bytes 1572868
  2105.0 193.8 %all-to-all-start.3 = ((bf16[3,1,1024,256]{3,0,1,2:T(4,128)(2,1)}), bf16[3,1,1024,256]{3,0,1,2:T(4,128)(2,1)S(1)}, u32[]{:S(2)}, u32[]{:S(2)}) async-start(bf16[3,1,1024,256]{3,0,1,2:T(4,128)(2,1)} %copy.210), calls=%async_computation.3 | async-start | bytes 4194304 | tf_op jit(solution)/shard_map/all_to_all | solution.py:311
  2108.8 171.5 %copy-start.5 = (f32[128,2048]{1,0:T(8,128)S(1)}, f32[128,2048]{1,0:T(8,128)}, u32[]{:S(2)}) copy-start(f32[128,2048]{1,0:T(8,128)} %copy-done.4) | copy-start | bytes 3145732
  2303.8 51.4 %copy-start.12 = (f32[128,2048]{1,0:T(8,128)S(1)}, f32[128,2048]{1,0:T(8,128)}, u32[]{:S(2)}) copy-start(f32[128,2048]{1,0:T(8,128)} %get-tuple-element.683) | copy-start | bytes 3145732
  2303.8 51.4 %copy-start.27 = (f32[128]{0:T(128)S(1)}, f32[128]{0:T(128)}, u32[]{:S(2)}) copy-start(f32[128]{0:T(128)} %get-tuple-element.711) | copy-start | bytes 1540
  (22 other events, 110.4 us)
Sparse Core Ops, SparseCore 0:
  9.8 230.2 all-gather.10
  242.0 87.4 all-gather.12
  331.4 576.6 all-gather.14
  909.8 297.0 all-gather.16
  1208.3 46.8 all-gather.18
  1257.3 56.9 all-gather.22
  1315.8 78.7 all-gather.20
  1396.2 135.9 all-gather.24
  1536.0 136.1 all-reduce.5
  1675.0 35.1 reduce-scatter.3
  1713.1 86.5 reduce-scatter.7
  1802.6 152.9 reduce-scatter.5
